TPU v7x, 32 devices: a whole 2x2x4 slice. The times are simulated.
32 devices in a mesh: ctx: 8 (over z, x), head: 4 (over y, core).
Axes of the slice: x: 2, y: 2, z: 4, core: 2. Of those that a mesh axis runs over, the one named last changes fastest.
Arguments:
- q_latent: bfloat16 [1024, 1536], P('ctx'), may hold values from -6 to 6
- latent_bias: float32 [8, 1536], P('ctx'), may hold values from -3 to 3
- norm_gain: float32 [1536], replicated, may hold values from 0.5 to 1.5
- w_q: bfloat16 [1536, 24576], P('ctx', 'head'), may hold values from -0.15625 to 0.15625
- steer: float32 [8, 24576], P('ctx', 'head'), may hold values from -10 to 10
- kv_latent: bfloat16 [1024, 512], P('ctx'), may hold values from -6 to 6
- key_rope: bfloat16 [1024, 64], P('ctx'), may hold values from -10 to 10
- w_uk: bfloat16 [512, 16384], P(None, 'head'), may hold values from -0.25 to 0.25
- w_uv: bfloat16 [512, 16384], P(None, 'head'), may hold values from -0.25 to 0.25
- d_out: bfloat16 [1024, 16384], P('ctx', 'head'), may hold values from -0.29882812 to 0.29882812
- block_mask: int32 [8, 8], replicated, may hold values from 0 to 1, as said below
Outputs:
- grad_steer: float32 [8, 24576], P('ctx', 'head')
- grad_latent_bias: float32 [8, 1536], P('ctx')
Inputs may be any that keep to these rules, and one draw needn't show every extreme that they name: `block_mask`: query block i always attends key block i; its other entries are 1 at a rate drawn per query block among 1/16, 2/16, 4/16 and 7/16.
All inputs are finite; a program needn't handle non-finite values.
Results may differ from a plain program's by a relative error of at most 0.024.
Values may be sent and summed in bfloat16 or wider, within the bound.
No kernel may reach another device: no remote copies, remote signals or barrier semaphores. Data moves between devices by JAX's collectives and lax.ppermute only.
A program may use at most 128 MiB of HBM per device.

v0:
```python
import math
import jax
import jax.numpy as jnp
from jax import lax
from jax.sharding import PartitionSpec as P

KVL = 512
NOPE = 128
ROPE = 64
VD = 128
BLK = 128
epsilon = 1e-06
lowest = -1e30


def contract_last(left, right):
    return lax.dot_general(
        left, right, (((1,), (1,)), ((), ())), preferred_element_type=jnp.float32
    )


def shards(
    q_latent, latent_bias, norm_gain, w_q, steer, kv_latent, key_rope, w_uk, w_uv, d_out, block_mask
):
    queries = q_latent.shape[0]
    nblocks = queries // BLK
    head_count = w_uk.shape[1] // NOPE
    head_width = NOPE + ROPE
    score_scale = head_width ** (-0.5)
    row_count = queries * head_count
    shifted = q_latent.astype(jnp.float32) + jnp.repeat(latent_bias, BLK, axis=0)
    inv_rms = lax.rsqrt(jnp.mean(shifted * shifted, axis=1, keepdims=True) + epsilon)
    normed = shifted * inv_rms
    c_query = (normed * norm_gain).astype(jnp.bfloat16)
    full_wq = lax.all_gather(w_q, "ctx", axis=0, tiled=True)
    projected = jnp.dot(c_query, full_wq, preferred_element_type=jnp.float32)
    query_all = (
        (projected + jnp.repeat(steer, BLK, axis=0))
        .astype(jnp.bfloat16)
        .reshape(queries, head_count, head_width)
    )
    q_rope = query_all[:, :, NOPE:].reshape(row_count, ROPE)
    key_up = w_uk.reshape(KVL, head_count, NOPE)
    value_up = w_uv.reshape(KVL, head_count, VD)
    q_absorbed = (
        jnp.einsum(
            "qhn,khn->qhk", query_all[:, :, :NOPE], key_up, preferred_element_type=jnp.float32
        )
        .astype(jnp.bfloat16)
        .reshape(row_count, KVL)
    )
    g_absorbed = (
        jnp.einsum(
            "qhv,khv->qhk",
            d_out.reshape(queries, head_count, VD),
            value_up,
            preferred_element_type=jnp.float32,
        )
        .astype(jnp.bfloat16)
        .reshape(row_count, KVL)
    )
    my_mask = lax.dynamic_slice_in_dim(block_mask, lax.axis_index("ctx") * nblocks, nblocks, 0)
    start_status = (
        jnp.full((row_count,), lowest, jnp.float32),
        jnp.zeros((row_count,), jnp.float32),
        jnp.zeros((row_count,), jnp.float32),
        jnp.zeros((2 * row_count, KVL), jnp.float32),
        jnp.zeros((2 * row_count, ROPE), jnp.float32),
    )
    lat_portion = lax.all_gather(kv_latent, "ctx", axis=0, tiled=True)
    rope_portion = lax.all_gather(key_rope, "ctx", axis=0, tiled=True)
    key_total = lat_portion.shape[0]
    tile_len = math.gcd(key_total, BLK)
    tile_count = key_total // tile_len

    def visit_tile(status, inputs):
        lat_tile, rope_tile, offset = inputs
        key_block = offset * tile_len // BLK
        column = lax.dynamic_index_in_dim(my_mask, key_block, 1, keepdims=False)

        def update(status):
            peak, total_weight, weighted, lat_acc, rope_acc = status
            live_rows = jnp.repeat(column > 0, head_count * BLK)[:, None]
            scores = (
                contract_last(q_absorbed, lat_tile) + contract_last(q_rope, rope_tile)
            ) * score_scale
            scores = jnp.where(live_rows, scores, lowest)
            new_peak = jnp.maximum(peak, jnp.max(scores, axis=1))
            factor = jnp.exp(peak - new_peak)
            weights = jnp.where(live_rows, jnp.exp(scores - new_peak[:, None]), 0.0)
            dots = contract_last(g_absorbed, lat_tile)
            mixed = weights * dots
            total_weight = total_weight * factor + jnp.sum(weights, axis=1)
            weighted = weighted * factor + jnp.sum(mixed, axis=1)
            stacked = jnp.concatenate([mixed, weights], axis=0).astype(jnp.bfloat16)
            doubled = jnp.concatenate([factor, factor])[:, None]
            lat_acc = lat_acc * doubled + jnp.dot(
                stacked, lat_tile, preferred_element_type=jnp.float32
            )
            rope_acc = rope_acc * doubled + jnp.dot(
                stacked, rope_tile, preferred_element_type=jnp.float32
            )
            return (new_peak, total_weight, weighted, lat_acc, rope_acc)

        def keep_status(status):
            return status

        return (lax.cond(jnp.max(column) > 0, update, keep_status, status), None)

    offsets = jnp.arange(tile_count, dtype=jnp.int32)
    tiles = (
        lat_portion.reshape(tile_count, tile_len, KVL),
        rope_portion.reshape(tile_count, tile_len, ROPE),
        offsets,
    )
    result, unused = lax.scan(visit_tile, start_status, tiles)
    peak, total_weight, weighted, lat_acc, rope_acc = result
    ratio = (weighted / total_weight)[:, None]
    inverse = (score_scale / total_weight)[:, None]
    grad_lat = ((lat_acc[:row_count] - ratio * lat_acc[row_count:]) * inverse).astype(jnp.bfloat16)
    grad_rope = (rope_acc[:row_count] - ratio * rope_acc[row_count:]) * inverse
    grad_nope = jnp.einsum(
        "qhk,khn->qhn",
        grad_lat.reshape(queries, head_count, KVL),
        key_up,
        preferred_element_type=jnp.float32,
    )
    grad_query = jnp.concatenate(
        [grad_nope, grad_rope.reshape(queries, head_count, ROPE)], axis=2
    ).reshape(queries, head_count * head_width)
    grad_steer = jnp.sum(grad_query.reshape(nblocks, BLK, head_count * head_width), axis=1)
    grad_round = grad_query.astype(jnp.bfloat16)
    partial_grad = contract_last(grad_round, full_wq)
    latent_grad = lax.psum(partial_grad.astype(jnp.bfloat16), "head").astype(jnp.float32)
    scaled = latent_grad * norm_gain
    project_mean = jnp.mean(scaled * normed, axis=1, keepdims=True)
    grad_shifted = inv_rms * (scaled - normed * project_mean)
    grad_bias = jnp.sum(grad_shifted.reshape(nblocks, BLK, grad_shifted.shape[1]), axis=1)
    return (grad_steer, grad_bias)


def solution(mesh):
    in_specs = (
        P("ctx", None),
        P("ctx", None),
        P(),
        P("ctx", "head"),
        P("ctx", "head"),
        P("ctx", None),
        P("ctx", None),
        P(None, "head"),
        P(None, "head"),
        P("ctx", "head"),
        P(),
    )
    out_specs = (P("ctx", "head"), P("ctx", None))
    return jax.shard_map(shards, mesh=mesh, in_specs=in_specs, out_specs=out_specs, check_vma=False)
```

profile of v0, /device:TPU:0, one launch (start us, length us, event | category | flops | bytes accessed | tf_op | source)
XLA Modules:
  0.0 604.1 jit_solution(11395170812251532337)
XLA Ops:
  7.2 0.7 all-gather.5.cloned.1.call-update
  8.0 0.7 all-gather.3.cloned.1.call-update
  8.7 54.1 %all_gather.11 = bf16[1024,64]{0,1:T(8,128)(2,1)S(1)} all-gather(bf16[128,64]{0,1:T(8,128)(2,1)} %param.21), channel_id=1, replica_groups=mesh['ctx'=8,'head'=4] {'ctx'}, dimensions={0}, use_global_device_ids=true | all-gather | bytes 147456 | tf_op jit(solution)/shard_map/all_gather | solution.py:71
  62.9 6.5 %copy.46 = bf16[512,4096]{0,1:T(8,128)(2,1)} copy(bf16[512,4096]{1,0:T(8,128)(2,1)} %param.22) | data formatting | bytes 8388608 | tf_op jit(solution)/shard_map/reshape | solution.py:43
  69.4 3.5 convert_bitcast_fusion.1
  73.0 4.4 copy.40
  77.6 0.7 constant_dynamic-slice_fusion.1
  78.3 298.5 %all-gather.5.cloned.1.call-done = bf16[1536,6144]{1,0:T(8,128)(2,1)} async-done(((bf16[192,6144]{1,0:T(8,128)(2,1)}), bf16[1536,6144]{1,0:T(8,128)(2,1)}) %all-gather.5.cloned.1.call-update) | async-done | bytes 18874384 | tf_op jit(solution)/shard_map/all_gather | solution.py:35
  376.8 10.2 %fusion.23 = bf16[128,6144]{1,0:T(8,128)(2,1)} fusion(bf16[1536,6144]{1,0:T(8,128)(2,1)} %all-gather.5.cloned.1.call-done, f32[6144]{0:T(1024)S(1)} %bitcast.78, bf16[128,1536]{1,0:T(8,128)(2,1)S(1)} %copy-done.5, f32[1536]{0:T(1024)S(1)} %copy-done.9, f32[128]{0:T(128)S(1)} %add_rsqrt_fusion, f32[1536]{0:T(1024)S(1)} %reduce.7), kind=kOutput, calls=%fused_computation.37 | convolution fusion | flops 2418475008 | bytes 20877824 | tf_op jit(solution)/shard_map/dot_general | solution.py:36
  387.0 2.1 copy.32
  389.2 2.5 copy.37
  391.7 3.5 convert_bitcast_fusion.2
  395.2 4.5 copy.35
  399.7 18.9 %all-gather.3.cloned.1.call-done = bf16[1024,512]{1,0:T(8,128)(2,1)} async-done(((bf16[128,512]{1,0:T(8,128)(2,1)}), bf16[1024,512]{1,0:T(8,128)(2,1)}) %all-gather.3.cloned.1.call-update) | async-done | bytes 1048592 | tf_op jit(solution)/shard_map/all_gather | solution.py:70
  418.8 7.9 %broadcast_in_dim.47 = f32[8192,512]{1,0:T(8,128)} broadcast(f32[]{:T(128)} %constant.105.clone.1), dimensions={} | broadcast | bytes 16777220 | tf_op jit(solution)/shard_map/broadcast_in_dim | solution.py:67
  426.7 62.8 %while.20 = (s32[]{:T(128)}, f32[4096]{0:T(1024)S(1)}, f32[4096]{0:T(1024)S(1)}, f32[4096]{0:T(1024)S(1)}, f32[8192,512]{1,0:T(8,128)}, /*index=5*/f32[8192,64]{...) while((s32[]{:T(128)}, f32[4096]{0:T(1024)S(1)}, ...), condition=%wide.region_7.8_spmd, body=%wide.region_1.7_spmd.sunk | while | flops 2372423680 | bytes 79006344 | solution.py:116
  427.9 0.6 fusion.59
  429.2 21.2 %conditional.2 = ((f32[4096]{0:T(1024)S(1)}, f32[4096]{0:T(1024)S(1)}, f32[4096]{0:T(1024)S(1)}, f32[8192,512]{1,0:T(8,128)}, f32[8192,64]{0,1:T(8,128)S(1)})) conditional(s32[]{:T(128)} %bitcast.67, (f32[4096]{0:T(1024)S(1)}, f32[4096]{0:T(1024)S(1)}, f32[4096]{0:T(1024)S(1)}, f32[8192,512]{1,0:T(8,128)}, f32[8192,64]{0,1:T(8,128)S(1)}) %tuple.55, ...), branch_computations={%region_2.2_spmd, %region_3.6_spmd} | conditional | flops 2372423680 | bytes 79005792 | solution.py:108
  429.8 3.7 fusion.7
  433.6 1.9 fusion.43
  436.1 2.5 fusion.4
  438.6 0.9 convolution_add_fusion
  439.5 10.9 %multiply_add_fusion = f32[8192,512]{1,0:T(8,128)} fusion(f32[8192,512]{1,0:T(8,128)} %get-tuple-element.261, f32[8192]{0:T(1024)S(1)} %pad_maximum_fusion.3, bf16[4096,128]{0,1:T(8,128)(2,1)S(1)} %get-tuple-element.320, bf16[4096,128]{0,1:T(8,128)(2,1)S(1)} %get-tuple-element.327, bf16[8,128,512]{2,1,0:T(8,128)(2,1)} %get-tuple-element.253, ...), kind=kOutput, calls=%fused_computation | convolution fusion | flops 1086324736 | bytes 35815936 | tf_op jit(solution)/shard_map/while/body/eval_jaxpr/cond/branch_1_fun/dot_general | solution.py:97
  451.7 0.6 fusion.59
  454.2 0.6 fusion.59
  456.8 0.6 fusion.59
  459.4 0.6 fusion.59
  461.9 0.6 fusion.59
  464.5 0.6 fusion.59
  465.8 21.2 %conditional.2 = ((f32[4096]{0:T(1024)S(1)}, f32[4096]{0:T(1024)S(1)}, f32[4096]{0:T(1024)S(1)}, f32[8192,512]{1,0:T(8,128)}, f32[8192,64]{0,1:T(8,128)S(1)})) conditional(s32[]{:T(128)} %bitcast.67, (f32[4096]{0:T(1024)S(1)}, f32[4096]{0:T(1024)S(1)}, f32[4096]{0:T(1024)S(1)}, f32[8192,512]{1,0:T(8,128)}, f32[8192,64]{0,1:T(8,128)S(1)}) %tuple.55, ...), branch_computations={%region_2.2_spmd, %region_3.6_spmd} | conditional | flops 2372423680 | bytes 79005792 | solution.py:108
  466.4 3.7 fusion.7
  470.2 1.9 fusion.43
  472.7 2.5 fusion.4
  475.2 0.9 convolution_add_fusion
  476.1 10.9 %multiply_add_fusion = f32[8192,512]{1,0:T(8,128)} fusion(f32[8192,512]{1,0:T(8,128)} %get-tuple-element.261, f32[8192]{0:T(1024)S(1)} %pad_maximum_fusion.3, bf16[4096,128]{0,1:T(8,128)(2,1)S(1)} %get-tuple-element.320, bf16[4096,128]{0,1:T(8,128)(2,1)S(1)} %get-tuple-element.327, bf16[8,128,512]{2,1,0:T(8,128)(2,1)} %get-tuple-element.253, ...), kind=kOutput, calls=%fused_computation | convolution fusion | flops 1086324736 | bytes 35815936 | tf_op jit(solution)/shard_map/while/body/eval_jaxpr/cond/branch_1_fun/dot_general | solution.py:97
  488.2 0.6 fusion.59
  489.5 6.9 %multiply_convert_fusion = bf16[4096,512]{1,0:T(8,128)(2,1)S(1)} fusion(f32[8192,512]{1,0:T(8,128)} %get-tuple-element.288, f32[4096]{0:T(1024)S(1)} %get-tuple-element.331, f32[4096]{0:T(1024)S(1)} %get-tuple-element.330), kind=kLoop, calls=%fused_computation.35 | loop fusion | flops 8388608 | bytes 21004288 | tf_op jit(solution)/shard_map/convert_element_type | solution.py:120
  496.6 2.8 fusion.33
  499.3 1.9 copy.43
  501.3 2.7 copy.44
  503.9 1.0 copy-done.4
  504.9 1.4 fusion.31
  506.3 14.1 %convolution_convert_fusion = bf16[128,1536]{1,0:T(8,128)(2,1)} fusion(bf16[128,6144]{0,1:T(8,128)(2,1)} %bitcast.76, bf16[1536,6144]{1,0:T(8,128)(2,1)} %all-gather.5.cloned.1.call-done), kind=kOutput, calls=%fused_computation.48 | convolution fusion | flops 2416115712 | bytes 20840448 | tf_op jit(solution)/shard_map/dot_general | solution.py:17
  520.5 3.0 fusion.32
  523.5 1.5 reduce_sum.64
  524.9 69.5 %all-reduce.2.cloned.1.call-done = bf16[128,1536]{1,0:T(8,128)(2,1)} async-done(((bf16[128,1536]{1,0:T(8,128)(2,1)}), bf16[128,1536]{1,0:T(8,128)(2,1)}) %all-reduce.2.cloned.1.call-update) | async-done | bytes 393232 | tf_op jit(solution)/shard_map/psum | solution.py:134
  594.4 1.3 multiply_reduce_fusion.1
  595.7 1.3 multiply_reduce_fusion
  (71 shorter events, 7.7 us)
Async XLA Ops:
  7.2 62.3 %copy-start = (bf16[128,4096]{1,0:T(8,128)(2,1)S(1)}, bf16[128,4096]{1,0:T(8,128)(2,1)}, u32[]{:S(2)}) copy-start(bf16[128,4096]{1,0:T(8,128)(2,1)} %param.24) | copy-start | bytes 3145732
  7.2 369.6 %all-gather.5.cloned.1.call-start = ((), (), s32[]{:S(2)}) async-start(), calls=%async_computation.1 | async-start | bytes 21233664 | tf_op jit(solution)/shard_map/all_gather | solution.py:35
  7.9 410.7 %all-gather.3.cloned.1.call-start = ((), (), s32[]{:S(2)}) async-start(), calls=%async_computation | async-start | bytes 1179648 | tf_op jit(solution)/shard_map/all_gather | solution.py:70
  8.7 585.8 %all-reduce.2.cloned.1.call-start = ((), (), s32[]{:S(2)}) async-start(), calls=%async_computation.2 | async-start | bytes 786432 | tf_op jit(solution)/shard_map/psum | solution.py:134
  73.0 4.4 copy-start.13
  73.0 4.4 copy-start.5
  73.0 303.8 %copy-start.9 = (f32[1536]{0:T(1024)S(1)}, f32[1536]{0:T(1024)}, u32[]{:S(2)}) copy-start(f32[1536]{0:T(1024)} %param.17) | copy-start | bytes 18436
  73.0 303.8 %copy-start.11 = (f32[1,6144]{1,0:T(1,128)S(1)}, f32[1,6144]{1,0:T(1,128)}, u32[]{:S(2)}) copy-start(f32[1,6144]{1,0:T(1,128)} %param.19) | copy-start | bytes 73732
  77.4 309.6 %copy-start.7 = (f32[1536]{0:T(1024)}, f32[1536]{0:T(1024)S(1)}, u32[]{:S(2)}) copy-start(f32[1536]{0:T(1024)S(1)} %reduce.7) | copy-start | bytes 18436
  78.3 308.7 %copy-start.12 = (f32[128]{0:T(128)}, f32[128]{0:T(128)S(1)}, u32[]{:S(2)}) copy-start(f32[128]{0:T(128)S(1)} %add_rsqrt_fusion) | copy-start | bytes 1540
  433.6 2.5 copy-start.2
  470.2 2.5 copy-start.2
  489.5 7.0 %copy-start.3 = (bf16[512,4096]{0,1:T(8,128)(2,1)S(1)}, bf16[512,4096]{0,1:T(8,128)(2,1)}, u32[]{:S(2)}) copy-start(bf16[512,4096]{0,1:T(8,128)(2,1)} %copy.46) | copy-start | bytes 12582916
  503.9 1.0 copy-start.4
  506.3 88.1 %copy-start.6 = (bf16[128,1536]{1,0:T(8,128)(2,1)S(1)}, bf16[128,1536]{1,0:T(8,128)(2,1)}, u32[]{:S(2)}) copy-start(bf16[128,1536]{1,0:T(8,128)(2,1)} %param.15) | copy-start | bytes 1179652
  506.3 88.1 %copy-start.8 = (f32[1536]{0:T(1024)S(1)}, f32[1536]{0:T(1024)}, u32[]{:S(2)}) copy-start(f32[1536]{0:T(1024)} %copy-done.7) | copy-start | bytes 18436
  506.3 88.1 %copy-start.10 = (f32[1536]{0:T(1024)S(1)}, f32[1536]{0:T(1024)}, u32[]{:S(2)}) copy-start(f32[1536]{0:T(1024)} %param.17) | copy-start | bytes 18436
  506.3 91.3 %copy-start.1 = (bf16[128,4096]{1,0:T(8,128)(2,1)S(1)}, bf16[128,4096]{1,0:T(8,128)(2,1)}, u32[]{:S(2)}) copy-start(bf16[128,4096]{1,0:T(8,128)(2,1)} %param.24) | copy-start | bytes 3145732
Sparse Core Ops, SparseCore 0:
  9.5 367.2 all-gather.4
  378.9 39.6 all-gather.2
  520.6 73.7 all-reduce.1
where the time goes:
time: 605 us; the launch traced here: 604 us
  waiting for transfers between devices  388 us (64%)
  matrix products  73.8 us (12%)
  blocking collectives  54.1 us (9%)
  local copies, waits for them, and re-layouts  42.6 us (7%)
  other arithmetic  19.1 us (3%)
  between operations  13.9 us (2%)
  loops' own time  12.1 us (2%)
    all_gather x1, waiting for transfers between devices, shards(): full_wq = lax.all_gather(w_q, 'ctx', axis=0, tiled=True)  298 us
    psum x1, waiting for transfers between devices, shards(): lax.psum(partial_grad.astype(jnp.bfloat16), 'head').astype(jnp.float32)  69.5 us
    all_gather x1, blocking collectives, shards(): rope_portion = lax.all_gather(key_rope, 'ctx', axis=0, tiled=True)  54.1 us
    dot_general x7, matrix products, contract_last(): lax.dot_general(left, right, (((1,), (1,)), ((), ())), preferred_element_...  30.3 us
    dot_general x2, matrix products, update(): jnp.dot(stacked, lat_tile, preferred_element_type=jnp.float32)  21.7 us
    all_gather x1, waiting for transfers between devices, shards(): lat_portion = lax.all_gather(kv_latent, 'ctx', axis=0, tiled=True)  18.9 us
  transfers between devices with their start and end apart: 3, of which 3 were waited for; matrix products, arithmetic and copies ran while one was open for 7% of the time, Pallas kernels for 0%

commit v1 on v0

--- a/solution.py
+++ b/solution.py
@@ -67,8 +67,12 @@
         jnp.zeros((2 * row_count, KVL), jnp.float32),
         jnp.zeros((2 * row_count, ROPE), jnp.float32),
     )
-    lat_portion = lax.all_gather(kv_latent, "ctx", axis=0, tiled=True)
-    rope_portion = lax.all_gather(key_rope, "ctx", axis=0, tiled=True)
+    keep_up_kinds = lambda slab_in, x0: jnp.split(
+        lax.all_gather(jnp.concatenate([slab_in, x0], 1), "ctx", axis=0, tiled=True),
+        [slab_in.shape[1]],
+        1,
+    )
+    lat_portion, rope_portion = keep_up_kinds(kv_latent, key_rope)
     key_total = lat_portion.shape[0]
     tile_len = math.gcd(key_total, BLK)
     tile_count = key_total // tile_len

time: 605 us -> 627 us (1.036)
  waiting for transfers between devices: 388 us -> 460 us
  blocking collectives: 54.1 us -> 0 us
    all_gather x1, waiting for transfers between devices: 298 us -> 360 us  [shards(): full_wq = lax.all_gather(w_q, 'ctx', axis=0, tiled=True)]
    all_gather x1 -> x0, blocking collectives: 54.1 us -> none  [shards(): rope_portion = lax.all_gather(key_rope, 'ctx', axis=0, tiled=True)]
    all_gather x1, waiting for transfers between devices: 18.9 us -> 28.9 us  [shards(): lax.all_gather(jnp.concatenate([slab_in, x0], 1), 'ctx', axis=0, tiled=True)]
  transfers between devices with their start and end apart: 3 -> 3, of which waited for: 3 -> 3; matrix products, arithmetic and copies ran while one was open for 7% -> 4% of each run, Pallas kernels for 0% -> 0%
where the time goes in v1:
time: 627 us; the launch traced here: 626 us
  waiting for transfers between devices  460 us (73%)
  matrix products  71 us (11%)
  local copies, waits for them, and re-layouts  46.6 us (7%)
  other arithmetic  20.9 us (3%)
  between operations  14 us (2%)
  loops' own time  12.7 us (2%)
    all_gather x1, waiting for transfers between devices, shards(): full_wq = lax.all_gather(w_q, 'ctx', axis=0, tiled=True)  360 us
    psum x1, waiting for transfers between devices, shards(): lax.psum(partial_grad.astype(jnp.bfloat16), 'head').astype(jnp.float32)  71.3 us
    all_gather x1, waiting for transfers between devices, shards(): lax.all_gather(jnp.concatenate([slab_in, x0], 1), 'ctx', axis=0, tiled=True)  28.9 us
    dot_general x7, matrix products, contract_last(): lax.dot_general(left, right, (((1,), (1,)), ((), ())), preferred_element_...  27.6 us
    dot_general x2, matrix products, update(): jnp.dot(stacked, lat_tile, preferred_element_type=jnp.float32)  21.7 us
  transfers between devices with their start and end apart: 3, of which 3 were waited for; matrix products, arithmetic and copies ran while one was open for 4% of the time, Pallas kernels for 0%

profile of v1, /device:TPU:0, one launch (start us, length us, event | category | flops | bytes accessed | tf_op | source)
XLA Modules:
  0.0 625.7 jit_solution(10141913895870668804)
XLA Ops:
  7.2 0.9 copy.32
  8.1 1.6 pad_maximum_fusion.5
  9.8 0.7 all-gather.5.cloned.1.call-update
  10.6 6.5 %copy.46 = bf16[512,4096]{0,1:T(8,128)(2,1)} copy(bf16[512,4096]{1,0:T(8,128)(2,1)} %param.22) | data formatting | bytes 8388608 | tf_op jit(solution)/shard_map/reshape | solution.py:43
  17.0 3.5 convert_bitcast_fusion.1
  20.5 4.4 copy.40
  25.0 0.7 constant_dynamic-slice_fusion.1
  25.9 28.9 %all-gather.3.cloned.1.call-done = bf16[1024,576]{1,0:T(8,128)(2,1)} async-done(((bf16[128,576]{1,0:T(8,128)(2,1)}), bf16[1024,576]{1,0:T(8,128)(2,1)}) %all-gather.3.cloned.1.call-update) | async-done | bytes 1179664 | tf_op jit(solution)/shard_map/all_gather | solution.py:71
  54.8 1.0 split.9
  55.7 2.3 split.8
  58.0 359.5 %all-gather.5.cloned.1.call-done = bf16[1536,6144]{1,0:T(8,128)(2,1)} async-done(((bf16[192,6144]{1,0:T(8,128)(2,1)}), bf16[1536,6144]{1,0:T(8,128)(2,1)}) %all-gather.5.cloned.1.call-update) | async-done | bytes 18874384 | tf_op jit(solution)/shard_map/all_gather | solution.py:35
  417.6 10.2 %fusion.23 = bf16[128,6144]{1,0:T(8,128)(2,1)} fusion(bf16[1536,6144]{1,0:T(8,128)(2,1)} %all-gather.5.cloned.1.call-done, f32[6144]{0:T(1024)S(1)} %bitcast.80, bf16[128,1536]{1,0:T(8,128)(2,1)S(1)} %copy-done.5, f32[1536]{0:T(1024)S(1)} %copy-done.9, f32[128]{0:T(128)S(1)} %add_rsqrt_fusion, f32[1536]{0:T(1024)S(1)} %reduce.7), kind=kOutput, calls=%fused_computation.37 | convolution fusion | flops 2418475008 | bytes 20877824 | tf_op jit(solution)/shard_map/dot_general | solution.py:36
  427.8 2.1 copy.33
  429.9 1.6 copy.37
  431.6 3.5 convert_bitcast_fusion.2
  435.0 4.5 copy.36
  439.7 7.9 %broadcast_in_dim.47 = f32[8192,512]{1,0:T(8,128)} broadcast(f32[]{:T(128)} %constant.105.clone.1), dimensions={} | broadcast | bytes 16777220 | tf_op jit(solution)/shard_map/broadcast_in_dim | solution.py:67
  447.6 63.6 %while.20 = (s32[]{:T(128)}, f32[4096]{0:T(1024)S(1)}, f32[4096]{0:T(1024)S(1)}, f32[4096]{0:T(1024)S(1)}, f32[8192,512]{1,0:T(8,128)}, /*index=5*/f32[8192,64]{...) while((s32[]{:T(128)}, f32[4096]{0:T(1024)S(1)}, ...), condition=%wide.region_7.8_spmd, body=%wide.region_1.7_spmd.sunk | while | flops 2372423680 | bytes 79530632 | solution.py:120
  449.0 0.7 fusion.59
  450.3 20.9 %conditional.2 = ((f32[4096]{0:T(1024)S(1)}, f32[4096]{0:T(1024)S(1)}, f32[4096]{0:T(1024)S(1)}, f32[8192,512]{1,0:T(8,128)}, f32[8192,64]{0,1:T(8,128)S(1)})) conditional(s32[]{:T(128)} %bitcast.67, (f32[4096]{0:T(1024)S(1)}, f32[4096]{0:T(1024)S(1)}, f32[4096]{0:T(1024)S(1)}, f32[8192,512]{1,0:T(8,128)}, f32[8192,64]{0,1:T(8,128)S(1)}) %tuple.55, ...), branch_computations={%region_2.2_spmd, %region_3.6_spmd} | conditional | flops 2372423680 | bytes 79530080 | solution.py:112
  451.0 3.7 fusion.7
  455.3 1.6 copy-done.2
  456.9 2.5 fusion.4
  459.4 0.9 convolution_add_fusion
  460.3 10.9 %multiply_add_fusion = f32[8192,512]{1,0:T(8,128)} fusion(f32[8192,512]{1,0:T(8,128)} %get-tuple-element.261, f32[8192]{0:T(1024)S(1)} %pad_maximum_fusion.3, bf16[4096,128]{0,1:T(8,128)(2,1)S(1)} %get-tuple-element.320, bf16[4096,128]{0,1:T(8,128)(2,1)S(1)} %get-tuple-element.327, bf16[8,128,512]{2,1,0:T(8,128)(2,1)} %get-tuple-element.253, ...), kind=kOutput, calls=%fused_computation | convolution fusion | flops 1086324736 | bytes 35815936 | tf_op jit(solution)/shard_map/while/body/eval_jaxpr/cond/branch_1_fun/dot_general | solution.py:101
  472.6 0.7 fusion.59
  475.3 0.7 fusion.59
  478.0 0.7 fusion.59
  480.7 0.7 fusion.59
  483.5 0.7 fusion.59
  486.2 0.7 fusion.59
  487.5 20.9 %conditional.2 = ((f32[4096]{0:T(1024)S(1)}, f32[4096]{0:T(1024)S(1)}, f32[4096]{0:T(1024)S(1)}, f32[8192,512]{1,0:T(8,128)}, f32[8192,64]{0,1:T(8,128)S(1)})) conditional(s32[]{:T(128)} %bitcast.67, (f32[4096]{0:T(1024)S(1)}, f32[4096]{0:T(1024)S(1)}, f32[4096]{0:T(1024)S(1)}, f32[8192,512]{1,0:T(8,128)}, f32[8192,64]{0,1:T(8,128)S(1)}) %tuple.55, ...), branch_computations={%region_2.2_spmd, %region_3.6_spmd} | conditional | flops 2372423680 | bytes 79530080 | solution.py:112
  488.2 3.7 fusion.7
  492.5 1.6 copy-done.2
  494.1 2.5 fusion.4
  496.7 0.9 convolution_add_fusion
  497.6 10.9 %multiply_add_fusion = f32[8192,512]{1,0:T(8,128)} fusion(f32[8192,512]{1,0:T(8,128)} %get-tuple-element.261, f32[8192]{0:T(1024)S(1)} %pad_maximum_fusion.3, bf16[4096,128]{0,1:T(8,128)(2,1)S(1)} %get-tuple-element.320, bf16[4096,128]{0,1:T(8,128)(2,1)S(1)} %get-tuple-element.327, bf16[8,128,512]{2,1,0:T(8,128)(2,1)} %get-tuple-element.253, ...), kind=kOutput, calls=%fused_computation | convolution fusion | flops 1086324736 | bytes 35815936 | tf_op jit(solution)/shard_map/while/body/eval_jaxpr/cond/branch_1_fun/dot_general | solution.py:101
  511.2 6.9 %multiply_convert_fusion = bf16[4096,512]{1,0:T(8,128)(2,1)S(1)} fusion(f32[8192,512]{1,0:T(8,128)} %get-tuple-element.288, f32[4096]{0:T(1024)S(1)} %get-tuple-element.331, f32[4096]{0:T(1024)S(1)} %get-tuple-element.330), kind=kLoop, calls=%fused_computation.35 | loop fusion | flops 8388608 | bytes 21004288 | tf_op jit(solution)/shard_map/convert_element_type | solution.py:124
  518.2 2.8 fusion.33
  521.0 2.0 copy.43
  523.0 2.7 copy.44
  525.7 1.4 fusion.31
  527.2 14.1 %convolution_convert_fusion = bf16[128,1536]{1,0:T(8,128)(2,1)} fusion(bf16[128,6144]{0,1:T(8,128)(2,1)} %bitcast.78, bf16[1536,6144]{1,0:T(8,128)(2,1)} %all-gather.5.cloned.1.call-done), kind=kOutput, calls=%fused_computation.48 | convolution fusion | flops 2416115712 | bytes 20840448 | tf_op jit(solution)/shard_map/dot_general | solution.py:17
  541.3 2.8 fusion.32
  544.0 0.7 reduce_sum.64
  544.7 71.3 %all-reduce.2.cloned.1.call-done = bf16[128,1536]{1,0:T(8,128)(2,1)} async-done(((bf16[128,1536]{1,0:T(8,128)(2,1)}), bf16[128,1536]{1,0:T(8,128)(2,1)}) %all-reduce.2.cloned.1.call-update) | async-done | bytes 393232 | tf_op jit(solution)/shard_map/psum | solution.py:138
  616.0 1.3 multiply_reduce_fusion.1
  617.3 1.3 multiply_reduce_fusion
  (75 shorter events, 8.5 us)
Async XLA Ops:
  7.2 9.9 %copy-start = (bf16[128,4096]{1,0:T(8,128)(2,1)S(1)}, bf16[128,4096]{1,0:T(8,128)(2,1)}, u32[]{:S(2)}) copy-start(bf16[128,4096]{1,0:T(8,128)(2,1)} %param.24) | copy-start | bytes 3145732
  7.2 47.6 %all-gather.3.cloned.1.call-start = ((), (), s32[]{:S(2)}) async-start(), calls=%async_computation | async-start | bytes 1474560 | tf_op jit(solution)/shard_map/all_gather | solution.py:71
  9.8 407.8 %all-gather.5.cloned.1.call-start = ((), (), s32[]{:S(2)}) async-start(), calls=%async_computation.1 | async-start | bytes 21233664 | tf_op jit(solution)/shard_map/all_gather | solution.py:35
  10.5 605.5 %all-reduce.2.cloned.1.call-start = ((), (), s32[]{:S(2)}) async-start(), calls=%async_computation.2 | async-start | bytes 786432 | tf_op jit(solution)/shard_map/psum | solution.py:138
  20.5 4.4 copy-start.14
  20.5 5.1 copy-start.5
  20.5 397.0 %copy-start.9 = (f32[1536]{0:T(1024)S(1)}, f32[1536]{0:T(1024)}, u32[]{:S(2)}) copy-start(f32[1536]{0:T(1024)} %param.17) | copy-start | bytes 18436
  20.5 397.0 %copy-start.11 = (f32[1,6144]{1,0:T(1,128)S(1)}, f32[1,6144]{1,0:T(1,128)}, u32[]{:S(2)}) copy-start(f32[1,6144]{1,0:T(1,128)} %param.19) | copy-start | bytes 73732
  24.9 402.8 %copy-start.7 = (f32[1536]{0:T(1024)}, f32[1536]{0:T(1024)S(1)}, u32[]{:S(2)}) copy-start(f32[1536]{0:T(1024)S(1)} %reduce.7) | copy-start | bytes 18436
  25.8 401.9 %copy-start.12 = (f32[128]{0:T(128)}, f32[128]{0:T(128)S(1)}, u32[]{:S(2)}) copy-start(f32[128]{0:T(128)S(1)} %add_rsqrt_fusion) | copy-start | bytes 1540
  454.7 2.2 copy-start.2
  492.0 2.2 copy-start.2
  511.2 7.0 %copy-start.3 = (bf16[512,4096]{0,1:T(8,128)(2,1)S(1)}, bf16[512,4096]{0,1:T(8,128)(2,1)}, u32[]{:S(2)}) copy-start(bf16[512,4096]{0,1:T(8,128)(2,1)} %copy.46) | copy-start | bytes 12582916
  521.0 6.1 copy-start.4
  527.1 88.9 %copy-start.6 = (bf16[128,1536]{1,0:T(8,128)(2,1)S(1)}, bf16[128,1536]{1,0:T(8,128)(2,1)}, u32[]{:S(2)}) copy-start(bf16[128,1536]{1,0:T(8,128)(2,1)} %param.15) | copy-start | bytes 1179652
  527.1 88.9 %copy-start.8 = (f32[1536]{0:T(1024)S(1)}, f32[1536]{0:T(1024)}, u32[]{:S(2)}) copy-start(f32[1536]{0:T(1024)} %copy-done.7) | copy-start | bytes 18436
  527.1 88.9 %copy-start.10 = (f32[1536]{0:T(1024)S(1)}, f32[1536]{0:T(1024)}, u32[]{:S(2)}) copy-start(f32[1536]{0:T(1024)} %param.17) | copy-start | bytes 18436
  527.1 88.9 %copy-start.13 = (f32[128]{0:T(128)S(1)}, f32[128]{0:T(128)}, u32[]{:S(2)}) copy-start(f32[128]{0:T(128)} %copy-done.12) | copy-start | bytes 1540
  527.1 92.1 %copy-start.1 = (bf16[128,4096]{1,0:T(8,128)(2,1)S(1)}, bf16[128,4096]{1,0:T(8,128)(2,1)}, u32[]{:S(2)}) copy-start(bf16[128,4096]{1,0:T(8,128)(2,1)} %param.24) | copy-start | bytes 3145732
Sparse Core Ops, SparseCore 0:
  10.2 44.5 all-gather.2
  56.3 361.2 all-gather.4
  541.4 74.5 all-reduce.1
